TPU v7x, 512 devices: a whole 4x8x8 slice. The times are simulated.
512 devices in a mesh: req: 128 (over z_hi, x, y), tp: 4 (over z_lo, core).
Axes of the slice: x: 4, y: 8, z: 8 (z_hi: 4, z_lo: 2; z = z_hi * 2 + z_lo), core: 2. Of those that a mesh axis runs over, the one named last changes fastest.
Arguments:
- queries: bfloat16 [2, 1024, 2304], P(None, 'req', 'tp'), may hold values from -10 to 10
- new_keys: bfloat16 [2, 1024, 2304], P(None, 'req', 'tp'), may hold values from -4 to 4
- new_values: bfloat16 [2, 1024, 2304], P(None, 'req', 'tp'), may hold values from -4 to 4
- cache_keys: bfloat16 [32768, 2304], P('req', 'tp'), may hold values from -10 to 10
- cache_values: bfloat16 [32768, 2304], P('req', 'tp'), may hold values from -4 to 4
- lengths: int32 [128, 16], P('req'), may hold values from 1 to 128, 256 in all within a row
- hidden: bfloat16 [2, 1024, 2304], P(None, 'req'), may hold values from -6 to 6
- gain: float32 [2304], replicated, may hold values from 0.5 to 1.5
- expert_ids: int32 [2, 1024, 2], P(None, 'req'), may hold values from 0 to 7, all different within a row; in each aligned block of 8 rows (0 to 7, 8 to 15, ..., all dimensions but the last counted through in order) at most 3 rows name the same one
- route_weights: float32 [2, 1024, 2], P(None, 'req'), may hold values from 0.2 to 1
- old_place: int32 [128], replicated, may hold values from 0 to 63, as said below
- new_place: int32 [128], replicated, may hold values from 0 to 63, as said below
- old_weights: bfloat16 [128, 2304, 1728], P('req', None, 'tp'), as said below
Outputs:
- context: bfloat16 [2, 1024, 2304], P(None, 'req', 'tp')
- layer_out: bfloat16 [2, 1024, 2304], P(None, 'req', 'tp')
- new_weights: bfloat16 [128, 2304, 1728], P('req', None, 'tp')
Inputs may be any that keep to these rules, and one draw needn't show every extreme that they name: `old_place`: every one of the 64 shards is held by at least one device; the others hold duplicates. `new_place`: every one of the 64 shards is held by at least one device; the others hold duplicates. `old_weights`: devices with equal old_place hold equal weights. `expert_ids`: in a batch, the 8 tokens of one device name one expert at most 3 times, and each token names distinct experts. `lengths`: each row sums to 256.
All inputs are finite; a program needn't handle non-finite values.
Results may differ from a plain program's by a relative error of at most 0.009.
Values may be sent and summed in bfloat16 or wider, within the bound.
A program may use at most 64 MiB of HBM per device.

v0:
```python
import jax
import jax.numpy as jnp
from jax import lax
from jax.sharding import PartitionSpec as P

HEAD_SIZE = 64
EXPERTS = 8
CAP = 3


def attend(queries, new_keys, new_values, cache_keys, cache_values, lengths):
    batches, tok_rows, width = queries.shape
    heads = width // HEAD_SIZE
    pool = cache_keys.shape[0]
    scale = HEAD_SIZE ** (-0.5)
    req_lengths = lengths.reshape(-1)
    starts = jnp.cumsum(req_lengths) - req_lengths
    position = jnp.arange(pool, dtype=jnp.int32)
    owned = (position[None, :] >= starts[:, None]) & (
        position[None, :] < (starts + req_lengths)[:, None]
    )
    query_rows = queries.reshape(batches * tok_rows, heads, HEAD_SIZE)
    own_keys = new_keys.reshape(batches * tok_rows, heads, HEAD_SIZE)
    own_values = new_values.reshape(batches * tok_rows, heads, HEAD_SIZE)
    pool_keys = cache_keys.reshape(pool, heads, HEAD_SIZE)
    pool_values = cache_values.reshape(pool, heads, HEAD_SIZE)
    scores = (
        jnp.einsum("qhd,phd->hqp", query_rows, pool_keys, preferred_element_type=jnp.float32)
        * scale
    )
    scores = jnp.where(owned[None], scores, -jnp.inf)
    own_score = (
        jnp.einsum("qhd,qhd->hq", query_rows, own_keys, preferred_element_type=jnp.float32) * scale
    )
    highest = jnp.maximum(jnp.max(scores, axis=-1), own_score)
    exp_pool = jnp.exp(scores - highest[..., None])
    exp_own = jnp.exp(own_score - highest)
    denom = jnp.sum(exp_pool, axis=-1) + exp_own
    summed = jnp.einsum(
        "hqp,phd->qhd",
        exp_pool.astype(jnp.bfloat16),
        pool_values,
        preferred_element_type=jnp.float32,
    )
    prob_own = lax.optimization_barrier(exp_own.astype(jnp.bfloat16)).astype(jnp.float32)
    summed = summed + prob_own.T[:, :, None] * own_values.astype(jnp.float32)
    context = (summed / denom.T[:, :, None]).astype(jnp.bfloat16)
    return context.reshape(batches, tok_rows, width)


def choose_holders(place, me_index, nreq, shard_count):
    devices = jnp.arange(nreq, dtype=jnp.int32)
    holder = place[None, :] == jnp.arange(shard_count, dtype=jnp.int32)[:, None]
    before = (place[:, None] == place[None, :]) & (devices[:, None] < devices[None, :])
    rank_in = jnp.sum(before.astype(jnp.int32), axis=0)
    count = jnp.sum(holder.astype(jnp.int32), axis=1)
    wanted = me_index % count
    match = holder & (rank_in[None, :] == wanted[:, None])
    return jnp.sum(jnp.where(match, devices[None, :], 0), axis=1)


def expert_block(hidden_rows, chosen, weights_now, place, shard_weights, gain):
    nreq = lax.axis_size("req")
    me_index = lax.axis_index("req")
    split_count = max(1, nreq // 16)
    shard_count = EXPERTS * split_count
    tok_rows, width = hidden_rows.shape
    hid_dev = shard_weights.shape[1] // 3
    resid = hidden_rows.astype(jnp.float32)
    normed = (
        resid * gain / jnp.sqrt(jnp.mean(resid * resid, axis=-1, keepdims=True) + 1e-05)
    ).astype(jnp.bfloat16)
    flat_ids = chosen.reshape(-1)
    assigns = flat_ids.shape[0]
    shard_dest = choose_holders(place, me_index, nreq, shard_count)
    shard_list = flat_ids[:, None] * split_count + jnp.arange(split_count, dtype=jnp.int32)[None, :]
    pick = shard_list[:, :, None] == jnp.arange(shard_count, dtype=jnp.int32)[None, None, :]
    dest = jnp.sum(jnp.where(pick, shard_dest[None, None, :], 0), axis=-1)
    assign_index = jnp.arange(assigns, dtype=jnp.int32)
    earlier = (flat_ids[:, None] == flat_ids[None, :]) & (
        assign_index[None, :] < assign_index[:, None]
    )
    rank_in = jnp.sum(earlier.astype(jnp.int32), axis=1)
    slot = dest * CAP + rank_in[:, None]
    hits = jnp.any(
        slot[None, :, :] == jnp.arange(nreq * CAP, dtype=jnp.int32)[:, None, None], axis=-1
    )
    repeated = jnp.repeat(normed, assigns // tok_rows, axis=0)
    outgoing = jnp.dot(hits.astype(jnp.bfloat16), repeated, preferred_element_type=jnp.float32)
    outgoing = outgoing.astype(jnp.bfloat16).reshape(nreq, CAP, width)
    received = lax.all_to_all(outgoing, "req", split_axis=0, concat_axis=0, tiled=True)
    sources, items, feat = received.shape
    flat_rows = received.reshape(sources * items, feat)
    gate_up = jnp.dot(
        flat_rows, shard_weights[:, : 2 * hid_dev], preferred_element_type=jnp.float32
    )
    act = (jax.nn.silu(gate_up[:, :hid_dev]) * gate_up[:, hid_dev:]).astype(jnp.bfloat16)
    part = lax.dot_general(
        act,
        shard_weights[:, 2 * hid_dev :],
        (((1,), (1,)), ((), ())),
        preferred_element_type=jnp.float32,
    )
    part = part.astype(jnp.bfloat16).reshape(sources, items, feat)
    returned = lax.all_to_all(part, "req", split_axis=0, concat_axis=0, tiled=True)
    returned = returned.reshape(nreq * CAP, width)
    picked = (
        returned[slot.reshape(-1)]
        .astype(jnp.float32)
        .reshape(tok_rows, assigns // tok_rows, split_count, width)
    )
    partial_sum = jnp.einsum("rksd,rk->rd", picked, weights_now)
    tp_width = width // lax.axis_size("tp")
    tp_start = lax.axis_index("tp") * tp_width
    resid_share = lax.dynamic_slice_in_dim(resid, tp_start, tp_width, 1)
    whole = lax.psum(partial_sum.astype(jnp.bfloat16), "tp").astype(jnp.float32)
    share = lax.dynamic_slice_in_dim(whole, tp_start, tp_width, 1)
    return (resid_share + share).astype(jnp.bfloat16)


def migrate(old_weights, old_place, new_place):
    nreq = lax.axis_size("req")
    shard_count = EXPERTS * max(1, nreq // 16)
    _, width, columns = old_weights.shape
    piece = width // nreq
    pieces = old_weights.reshape(nreq, piece, columns)
    spread = lax.all_to_all(pieces, "req", split_axis=0, concat_axis=0, tiled=True)
    devices = jnp.arange(nreq, dtype=jnp.int32)
    shard_ids = jnp.arange(shard_count, dtype=jnp.int32)
    first_old = jnp.min(
        jnp.where(old_place[None, :] == shard_ids[:, None], devices[None, :], nreq), axis=1
    )
    needed = jnp.sum(
        jnp.where(new_place[:, None] == shard_ids[None, :], first_old[None, :], 0), axis=1
    )
    sending = spread[needed]
    collected = lax.all_to_all(sending, "req", split_axis=0, concat_axis=0, tiled=True)
    return collected.reshape(1, width, columns)


def on_device(
    queries,
    new_keys,
    new_values,
    cache_keys,
    cache_values,
    lengths,
    hidden,
    gain,
    expert_ids,
    route_weights,
    old_place,
    new_place,
    old_weights,
):
    context = attend(queries, new_keys, new_values, cache_keys, cache_values, lengths)
    moved = migrate(old_weights, old_place, new_place)
    first_out = expert_block(
        hidden[0], expert_ids[0], route_weights[0], old_place, old_weights[0], gain
    )
    second_out = expert_block(hidden[1], expert_ids[1], route_weights[1], new_place, moved[0], gain)
    layer_out = jnp.stack([first_out, second_out])
    return (context, layer_out, moved)


def solution(mesh):
    in_specs = (
        P(None, "req", "tp"),
        P(None, "req", "tp"),
        P(None, "req", "tp"),
        P("req", "tp"),
        P("req", "tp"),
        P("req", None),
        P(None, "req", None),
        P(),
        P(None, "req", None),
        P(None, "req", None),
        P(),
        P(),
        P("req", None, "tp"),
    )
    out_specs = (P(None, "req", "tp"), P(None, "req", "tp"), P("req", None, "tp"))
    return jax.shard_map(
        on_device, mesh=mesh, in_specs=in_specs, out_specs=out_specs, check_vma=False
    )
```

profile of v0, /device:TPU:1, one launch (start us, length us, event | category | flops | bytes accessed | tf_op | source)
XLA Modules:
  0.0 525.8 jit_solution(8682452073270853563)
XLA Ops:
  7.2 0.8 convert_reduce_fusion.4
  8.0 0.8 convert_reduce_fusion.2
  8.8 0.7 fusion.48
  9.9 0.9 fusion.27
  10.9 0.9 fusion.26
  11.9 0.8 convert_reduce_fusion.5
  12.8 0.8 select_reduce_fusion.4
  14.3 0.7 convolution_convert_fusion
  15.0 2.3 reshape.378
  17.2 20.8 %all-to-all-start.2 = ((bf16[128,3,2304]{2,1,0:T(4,128)(2,1)}), bf16[128,3,2304]{2,1,0:T(4,128)(2,1)S(1)}, u32[]{:S(2)}, u32[]{:S(2)}) async-start(bf16[128,3,2304]{2,1,0:T(4,128)(2,1)} %reshape.378), calls=%async_computation.2 | async-start | bytes 4718592 | tf_op jit(solution)/shard_map/all_to_all | solution.py:91
  38.1 4.1 copy.34
  42.1 5.2 reshape.380
  47.4 49.8 %all-to-all-done.2 = bf16[128,3,2304]{2,1,0:T(4,128)(2,1)S(1)} async-done(((bf16[128,3,2304]{2,1,0:T(4,128)(2,1)}), bf16[128,3,2304]{2,1,0:T(4,128)(2,1)S(1)}, u32[]{:S(2)}, u32[]{:S(2)}) %all-to-all-start.2) | async-done | bytes 1769504 | tf_op jit(solution)/shard_map/all_to_all | solution.py:91
  97.2 1.4 copy-done.1
  98.6 7.6 %all-to-all-start.3 = ((bf16[128,18,432]{2,1,0:T(8,128)(2,1)}), bf16[128,18,432]{2,1,0:T(8,128)(2,1)S(1)}, u32[]{:S(2)}, u32[]{:S(2)}) async-start(bf16[128,18,432]{2,1,0:T(8,128)(2,1)} %reshape.380), calls=%async_computation.3 | async-start | bytes 6291456 | tf_op jit(solution)/shard_map/all_to_all | solution.py:127
  106.4 0.7 broadcast_in_dim.84
  107.0 0.9 reshape.372
  109.1 1.9 convolution_convert_fusion.2
  111.0 5.4 %reshape.373 = bf16[128,3,2304]{2,1,0:T(4,128)(2,1)} reshape(bf16[384,2304]{1,0:T(8,128)(2,1)} %convolution_convert_fusion.2) | data formatting | bytes 3538944 | tf_op jit(solution)/shard_map/reshape | solution.py:90
  116.4 64.4 %all-to-all-done.3 = bf16[128,18,432]{2,1,0:T(8,128)(2,1)S(1)} async-done(((bf16[128,18,432]{2,1,0:T(8,128)(2,1)}), bf16[128,18,432]{2,1,0:T(8,128)(2,1)S(1)}, u32[]{:S(2)}, u32[]{:S(2)}) %all-to-all-start.3) | async-done | bytes 1990688 | tf_op jit(solution)/shard_map/all_to_all | solution.py:127
  180.8 8.4 %all-to-all-start = ((bf16[128,3,2304]{2,1,0:T(4,128)(2,1)}), bf16[128,3,2304]{2,1,0:T(4,128)(2,1)}, u32[]{:S(2)}, u32[]{:S(2)}) async-start(bf16[128,3,2304]{2,1,0:T(4,128)(2,1)} %reshape.373), calls=%async_computation | async-start | bytes 4718592 | tf_op jit(solution)/shard_map/all_to_all | solution.py:91
  189.3 2.4 gather_fusion.1
  191.7 53.7 %all-to-all-done = bf16[128,3,2304]{2,1,0:T(4,128)(2,1)} async-done(((bf16[128,3,2304]{2,1,0:T(4,128)(2,1)}), bf16[128,3,2304]{2,1,0:T(4,128)(2,1)}, u32[]{:S(2)}, u32[]{:S(2)}) %all-to-all-start) | async-done | bytes 1769504 | tf_op jit(solution)/shard_map/all_to_all | solution.py:91
  245.4 7.3 %all-to-all-start.4 = ((bf16[128,18,432]{2,1,0:T(8,128)(2,1)}), bf16[128,18,432]{2,1,0:T(8,128)(2,1)S(1)}, u32[]{:S(2)}, u32[]{:S(2)}) async-start(bf16[128,18,432]{2,1,0:T(8,128)(2,1)} %gather_fusion.1), calls=%async_computation.4 | async-start | bytes 6291456 | tf_op jit(solution)/shard_map/all_to_all | solution.py:137
  252.7 5.2 reshape.374
  257.9 2.7 fusion.2
  260.6 3.0 convolution_convert_fusion.1
  263.6 5.3 %reshape.375 = bf16[128,3,2304]{2,1,0:T(4,128)(2,1)} reshape(bf16[384,2304]{1,0:T(8,128)(2,1)} %convolution_convert_fusion.1) | data formatting | bytes 3538944 | tf_op jit(solution)/shard_map/reshape | solution.py:104
  269.0 55.9 %all-to-all-done.4 = bf16[128,18,432]{2,1,0:T(8,128)(2,1)S(1)} async-done(((bf16[128,18,432]{2,1,0:T(8,128)(2,1)}), bf16[128,18,432]{2,1,0:T(8,128)(2,1)S(1)}, u32[]{:S(2)}, u32[]{:S(2)}) %all-to-all-start.4) | async-done | bytes 1990688 | tf_op jit(solution)/shard_map/all_to_all | solution.py:137
  324.9 8.0 %all-to-all-start.1 = ((bf16[128,3,2304]{2,1,0:T(4,128)(2,1)}), bf16[128,3,2304]{2,1,0:T(4,128)(2,1)}, u32[]{:S(2)}, u32[]{:S(2)}) async-start(bf16[128,3,2304]{2,1,0:T(4,128)(2,1)} %reshape.375), calls=%async_computation.1 | async-start | bytes 4718592 | tf_op jit(solution)/shard_map/all_to_all | solution.py:105
  334.1 5.2 reshape.379
  339.2 2.6 squeeze_reshape.3
  341.8 3.1 fusion
  344.9 2.3 convolution_convert_fusion.3
  347.2 5.3 %reshape.381 = bf16[128,3,2304]{2,1,0:T(4,128)(2,1)} reshape(bf16[384,2304]{1,0:T(8,128)(2,1)} %convolution_convert_fusion.3) | data formatting | bytes 3538944 | tf_op jit(solution)/shard_map/reshape | solution.py:104
  352.6 33.7 %all-to-all-done.1 = bf16[128,3,2304]{2,1,0:T(4,128)(2,1)} async-done(((bf16[128,3,2304]{2,1,0:T(4,128)(2,1)}), bf16[128,3,2304]{2,1,0:T(4,128)(2,1)}, u32[]{:S(2)}, u32[]{:S(2)}) %all-to-all-start.1) | async-done | bytes 1769504 | tf_op jit(solution)/shard_map/all_to_all | solution.py:105
  386.3 7.9 %all-to-all-start.5 = ((bf16[128,3,2304]{2,1,0:T(4,128)(2,1)}), bf16[128,3,2304]{2,1,0:T(4,128)(2,1)}, u32[]{:S(2)}, u32[]{:S(2)}) async-start(bf16[128,3,2304]{2,1,0:T(4,128)(2,1)} %reshape.381), calls=%async_computation.5 | async-start | bytes 4718592 | tf_op jit(solution)/shard_map/all_to_all | solution.py:105
  394.5 0.7 copy.45
  395.2 0.7 copy.43
  396.1 0.7 reshape.367
  396.8 1.4 reshape.369
  398.3 1.0 fusion.14
  399.4 0.7 bitcast_subtract_fusion
  400.1 1.7 fusion.49
  401.8 1.5 reshape.384
  403.2 0.7 fusion.45
  403.9 0.7 fusion.43
  405.2 1.1 fusion.15
  407.5 0.7 slice_convert_fusion.1
  408.1 5.2 reshape.376
  413.3 4.2 gather_fusion
  417.5 1.5 convert_reduce_fusion.1
  419.9 26.4 %all-to-all-done.5 = bf16[128,3,2304]{2,1,0:T(4,128)(2,1)} async-done(((bf16[128,3,2304]{2,1,0:T(4,128)(2,1)}), bf16[128,3,2304]{2,1,0:T(4,128)(2,1)}, u32[]{:S(2)}, u32[]{:S(2)}) %all-to-all-start.5) | async-done | bytes 1769504 | tf_op jit(solution)/shard_map/all_to_all | solution.py:105
  446.3 5.2 reshape.382
  451.5 4.1 gather_fusion.2
  455.7 1.5 convert_reduce_fusion
  458.1 1.3 fusion.8
  459.5 0.7 reshape.371
  460.2 2.6 reshape.383
  462.8 4.1 copy.35
  466.9 49.8 %all-reduce.3.cloned.1.call-done = (bf16[8,2304]{1,0:T(8,128)(2,1)}, bf16[8,2304]{1,0:T(8,128)(2,1)}) async-done(((bf16[8,2304]{1,0:T(8,128)(2,1)}, bf16[8,2304]{1,0:T(8,128)(2,1)}), (bf16[8,2304]{1,0:T(8,128)(2,1)}, bf16[8,2304]{1,0:T(8,128)(2,1)})) %all-reduce.3.cloned.1.call-update) | async-done | bytes 73744 | tf_op jit(solution)/shard_map/psum | solution.py:116
  516.7 0.8 fusion.37
  517.5 0.8 fusion.38
  518.3 0.6 pad_maximum_fusion
  (70 shorter events, 8.2 us)
Async XLA Ops:
  7.2 392.9 %copy-start = (bf16[256,576]{0,1:T(8,128)(2,1)S(1)}, bf16[256,576]{0,1:T(8,128)(2,1)}, u32[]{:S(2)}) copy-start(bf16[256,576]{0,1:T(8,128)(2,1)} %param.16) | copy-start | bytes 884740
  17.2 79.9 %all-to-all-start.2 = ((bf16[128,3,2304]{2,1,0:T(4,128)(2,1)}), bf16[128,3,2304]{2,1,0:T(4,128)(2,1)S(1)}, u32[]{:S(2)}, u32[]{:S(2)}) async-start(bf16[128,3,2304]{2,1,0:T(4,128)(2,1)} %reshape.378), calls=%async_computation.2 | async-start | bytes 4718592 | tf_op jit(solution)/shard_map/all_to_all | solution.py:91
  47.4 60.8 %copy-start.9 = (s32[128]{0:T(128)S(1)}, s32[128]{0:T(128)}, u32[]{:S(2)}) copy-start(s32[128]{0:T(128)} %param.23) | copy-start | bytes 1540
  97.2 1.4 copy-start.1
  98.6 82.2 %all-to-all-start.3 = ((bf16[128,18,432]{2,1,0:T(8,128)(2,1)}), bf16[128,18,432]{2,1,0:T(8,128)(2,1)S(1)}, u32[]{:S(2)}, u32[]{:S(2)}) async-start(bf16[128,18,432]{2,1,0:T(8,128)(2,1)} %reshape.380), calls=%async_computation.3 | async-start | bytes 6291456 | tf_op jit(solution)/shard_map/all_to_all | solution.py:127
  116.4 72.8 %copy-start.12 = (s32[128]{0:T(128)S(1)}, s32[128]{0:T(128)}, u32[]{:S(2)}) copy-start(s32[128]{0:T(128)} %param.24) | copy-start | bytes 1540
  180.8 64.7 %all-to-all-start = ((bf16[128,3,2304]{2,1,0:T(4,128)(2,1)}), bf16[128,3,2304]{2,1,0:T(4,128)(2,1)}, u32[]{:S(2)}, u32[]{:S(2)}) async-start(bf16[128,3,2304]{2,1,0:T(4,128)(2,1)} %reshape.373), calls=%async_computation | async-start | bytes 4718592 | tf_op jit(solution)/shard_map/all_to_all | solution.py:91
  245.4 79.4 %all-to-all-start.4 = ((bf16[128,18,432]{2,1,0:T(8,128)(2,1)}), bf16[128,18,432]{2,1,0:T(8,128)(2,1)S(1)}, u32[]{:S(2)}, u32[]{:S(2)}) async-start(bf16[128,18,432]{2,1,0:T(8,128)(2,1)} %gather_fusion.1), calls=%async_computation.4 | async-start | bytes 6291456 | tf_op jit(solution)/shard_map/all_to_all | solution.py:137
  324.9 61.4 %all-to-all-start.1 = ((bf16[128,3,2304]{2,1,0:T(4,128)(2,1)}), bf16[128,3,2304]{2,1,0:T(4,128)(2,1)}, u32[]{:S(2)}, u32[]{:S(2)}) async-start(bf16[128,3,2304]{2,1,0:T(4,128)(2,1)} %reshape.375), calls=%async_computation.1 | async-start | bytes 4718592 | tf_op jit(solution)/shard_map/all_to_all | solution.py:105
  341.8 3.1 copy-start.2
  352.6 41.9 %copy-start.11 = (f32[2,8,2]{1,2,0:T(2,128)S(1)}, f32[2,8,2]{1,2,0:T(2,128)}, u32[]{:S(2)}) copy-start(f32[2,8,2]{1,2,0:T(2,128)} %param.22) | copy-start | bytes 388
  352.6 43.3 %copy-start.10 = (s32[1,16]{1,0:T(1,128)S(1)}, s32[1,16]{1,0:T(1,128)}, u32[]{:S(2)}) copy-start(s32[1,16]{1,0:T(1,128)} %param.18) | copy-start | bytes 196
  352.6 43.5 %copy-start.4 = (bf16[2,8,576]{2,1,0:T(8,128)(2,1)S(1)}, bf16[2,8,576]{2,1,0:T(8,128)(2,1)}, u32[]{:S(2)}) copy-start(bf16[2,8,576]{2,1,0:T(8,128)(2,1)} %param.13) | copy-start | bytes 55300
  352.6 54.9 %copy-start.3 = (bf16[2,8,2304]{2,1,0:T(8,128)(2,1)S(1)}, bf16[2,8,2304]{2,1,0:T(8,128)(2,1)}, u32[]{:S(2)}) copy-start(bf16[2,8,2304]{2,1,0:T(8,128)(2,1)} %param.19) | copy-start | bytes 221188
  386.3 60.0 %all-to-all-start.5 = ((bf16[128,3,2304]{2,1,0:T(4,128)(2,1)}), bf16[128,3,2304]{2,1,0:T(4,128)(2,1)}, u32[]{:S(2)}, u32[]{:S(2)}) async-start(bf16[128,3,2304]{2,1,0:T(4,128)(2,1)} %reshape.381), calls=%async_computation.5 | async-start | bytes 4718592 | tf_op jit(solution)/shard_map/all_to_all | solution.py:105
  394.2 122.5 %all-reduce.3.cloned.1.call-start = ((), (), s32[]{:S(2)}) async-start(), calls=%async_computation.6 | async-start | bytes 147456 | tf_op jit(solution)/shard_map/psum | solution.py:116
  413.3 5.7 %copy-start.8 = (bf16[8,2,1]{1,2,0:T(2,128)(2,1)S(1)}, bf16[8,2,1]{1,2,0:T(2,128)(2,1)}, u32[]{:S(2)}) copy-start(bf16[8,2,1]{1,2,0:T(2,128)(2,1)} %copy.43) | copy-start | bytes 100
  451.5 5.7 %copy-start.7 = (bf16[8,2,1]{1,2,0:T(2,128)(2,1)S(1)}, bf16[8,2,1]{1,2,0:T(2,128)(2,1)}, u32[]{:S(2)}) copy-start(bf16[8,2,1]{1,2,0:T(2,128)(2,1)} %copy.45) | copy-start | bytes 100
  451.5 6.5 %copy-start.5 = (f32[16,9]{0,1:T(8,128)S(1)}, f32[16,9]{0,1:T(8,128)}, u32[]{:S(2)}) copy-start(f32[16,9]{0,1:T(8,128)} %convert_bitcast_fusion) | copy-start | bytes 1732
  451.5 6.6 %copy-start.6 = (f32[16,9]{0,1:T(8,128)S(1)}, f32[16,9]{0,1:T(8,128)}, u32[]{:S(2)}) copy-start(f32[16,9]{0,1:T(8,128)} %fusion.40) | copy-start | bytes 1732
Sparse Core Ops, SparseCore 0:
  458.2 58.4 all-reduce.2
where the time goes:
time: 528 us; the launch traced here: 526 us
  waiting for transfers between devices  334 us (63%)
  local copies, waits for them, and re-layouts  81 us (15%)
  starting transfers between devices  60.2 us (11%)
  other arithmetic  19.5 us (4%)
  matrix products  17 us (3%)
  between operations  14.3 us (3%)
    all_to_all x2, waiting for transfers between devices, expert_block(): lax.all_to_all(outgoing, 'req', split_axis=0, concat_axis=0, tiled=True)  104 us
    all_to_all x1, waiting for transfers between devices, migrate(): lax.all_to_all(pieces, 'req', split_axis=0, concat_axis=0, tiled=True)  64.4 us
    all_to_all x2, waiting for transfers between devices, expert_block(): lax.all_to_all(part, 'req', split_axis=0, concat_axis=0, tiled=True)  60.1 us
    all_to_all x1, waiting for transfers between devices, migrate(): lax.all_to_all(sending, 'req', split_axis=0, concat_axis=0, tiled=True)  55.9 us
    psum x1, waiting for transfers between devices, expert_block(): whole = lax.psum(partial_sum.astype(jnp.bfloat16), 'tp').astype(jnp.float32)  49.8 us
    all_to_all x2, starting transfers between devices, expert_block(): lax.all_to_all(outgoing, 'req', split_axis=0, concat_axis=0, tiled=True)  29.2 us
    all_to_all x2, starting transfers between devices, expert_block(): lax.all_to_all(part, 'req', split_axis=0, concat_axis=0, tiled=True)  15.9 us
    reshape x2, local copies, waits for them, and re-layouts, expert_block(): part = part.astype(jnp.bfloat16).reshape(sources, items, feat)  10.7 us
  transfers between devices with their start and end apart: 7, of which 7 were waited for; matrix products, arithmetic and copies ran while one was open for 18% of the time, Pallas kernels for 0%

commit v1 on v0

--- a/solution.py
+++ b/solution.py
@@ -113,7 +113,9 @@
     tp_width = width // lax.axis_size("tp")
     tp_start = lax.axis_index("tp") * tp_width
     resid_share = lax.dynamic_slice_in_dim(resid, tp_start, tp_width, 1)
-    whole = lax.psum(partial_sum.astype(jnp.bfloat16), "tp").astype(jnp.float32)
+    whole = jnp.sum(lax.all_gather(partial_sum.astype(jnp.bfloat16), "tp"), axis=0).astype(
+        jnp.float32
+    )
     share = lax.dynamic_slice_in_dim(whole, tp_start, tp_width, 1)
     return (resid_share + share).astype(jnp.bfloat16)
 

time: 528 us -> 477 us (0.903)
  waiting for transfers between devices: 334 us -> 261 us
  blocking collectives: 0 us -> 43.5 us
  between operations: 14.3 us -> 0.95 us
  local copies, waits for them, and re-layouts: 81 us -> 74.9 us
    psum x1 -> x0, waiting for transfers between devices: 49.8 us -> none  [expert_block(): whole = lax.psum(partial_sum.astype(jnp.bfloat16), 'tp').astype(jnp.float32)]
    all_gather x0 -> x2, blocking collectives: none -> 43.5 us  [expert_block(): lax.all_gather(partial_sum.astype(jnp.bfloat16), 'tp')]
    all_to_all x2, waiting for transfers between devices: 60.1 us -> 34.1 us  [expert_block(): lax.all_to_all(part, 'req', split_axis=0, concat_axis=0, tiled=True)]
  transfers between devices with their start and end apart: 7 -> 6, of which waited for: 7 -> 5; matrix products, arithmetic and copies ran while one was open for 18% -> 19% of each run, Pallas kernels for 0% -> 0%
where the time goes in v1:
time: 477 us; the launch traced here: 475 us
  waiting for transfers between devices  261 us (55%)
  local copies, waits for them, and re-layouts  74.9 us (16%)
  starting transfers between devices  60.4 us (13%)
  blocking collectives  43.5 us (9%)
  other arithmetic  17.1 us (4%)
  matrix products  17 us (4%)
    all_to_all x2, waiting for transfers between devices, expert_block(): lax.all_to_all(outgoing, 'req', split_axis=0, concat_axis=0, tiled=True)  104 us
    all_to_all x1, waiting for transfers between devices, migrate(): lax.all_to_all(pieces, 'req', split_axis=0, concat_axis=0, tiled=True)  65 us
    all_to_all x1, waiting for transfers between devices, migrate(): lax.all_to_all(sending, 'req', split_axis=0, concat_axis=0, tiled=True)  58 us
    all_gather x2, blocking collectives, expert_block(): lax.all_gather(partial_sum.astype(jnp.bfloat16), 'tp')  43.5 us
    all_to_all x2, waiting for transfers between devices, expert_block(): lax.all_to_all(part, 'req', split_axis=0, concat_axis=0, tiled=True)  34.1 us
    all_to_all x2, starting transfers between devices, expert_block(): lax.all_to_all(outgoing, 'req', split_axis=0, concat_axis=0, tiled=True)  29 us
    all_to_all x2, starting transfers between devices, expert_block(): lax.all_to_all(part, 'req', split_axis=0, concat_axis=0, tiled=True)  15.5 us
    reshape x2, local copies, waits for them, and re-layouts, expert_block(): part = part.astype(jnp.bfloat16).reshape(sources, items, feat)  10.7 us
  transfers between devices with their start and end apart: 6, of which 5 were waited for; matrix products, arithmetic and copies ran while one was open for 19% of the time, Pallas kernels for 0%

profile of v1, /device:TPU:1, one launch (start us, length us, event | category | flops | bytes accessed | tf_op | source)
XLA Modules:
  0.0 475.0 jit_solution(3200980609622334973)
XLA Ops:
  0.6 0.8 convert_reduce_fusion.4
  1.5 0.8 convert_reduce_fusion.2
  2.3 0.7 fusion.48
  3.3 0.9 fusion.27
  4.3 0.9 fusion.26
  5.4 0.8 convert_reduce_fusion.5
  6.3 0.8 select_reduce_fusion.4
  7.8 0.7 convolution_convert_fusion
  8.4 2.3 reshape.378
  10.7 20.8 %all-to-all-start.2 = ((bf16[128,3,2304]{2,1,0:T(4,128)(2,1)}), bf16[128,3,2304]{2,1,0:T(4,128)(2,1)S(1)}, u32[]{:S(2)}, u32[]{:S(2)}) async-start(bf16[128,3,2304]{2,1,0:T(4,128)(2,1)} %reshape.378), calls=%async_computation.2 | async-start | bytes 4718592 | tf_op jit(solution)/shard_map/all_to_all | solution.py:91
  31.5 4.1 copy.34
  35.6 5.2 %reshape.380 = bf16[128,18,432]{2,1,0:T(8,128)(2,1)} reshape(bf16[1,2304,432]{2,1,0:T(8,128)(2,1)} %copy.34) | data formatting | bytes 3981312 | tf_op jit(solution)/shard_map/reshape | solution.py:128
  40.8 49.8 %all-to-all-done.2 = bf16[128,3,2304]{2,1,0:T(4,128)(2,1)S(1)} async-done(((bf16[128,3,2304]{2,1,0:T(4,128)(2,1)}), bf16[128,3,2304]{2,1,0:T(4,128)(2,1)S(1)}, u32[]{:S(2)}, u32[]{:S(2)}) %all-to-all-start.2) | async-done | bytes 1769504 | tf_op jit(solution)/shard_map/all_to_all | solution.py:91
  90.6 1.4 copy-done.1
  92.1 7.6 %all-to-all-start.3 = ((bf16[128,18,432]{2,1,0:T(8,128)(2,1)}), bf16[128,18,432]{2,1,0:T(8,128)(2,1)S(1)}, u32[]{:S(2)}, u32[]{:S(2)}) async-start(bf16[128,18,432]{2,1,0:T(8,128)(2,1)} %reshape.380), calls=%async_computation.3 | async-start | bytes 6291456 | tf_op jit(solution)/shard_map/all_to_all | solution.py:129
  99.8 0.7 broadcast_in_dim.84
  100.5 0.9 reshape.372
  102.6 1.9 convolution_convert_fusion.2
  104.5 5.4 %reshape.373 = bf16[128,3,2304]{2,1,0:T(4,128)(2,1)} reshape(bf16[384,2304]{1,0:T(8,128)(2,1)} %convolution_convert_fusion.2) | data formatting | bytes 3538944 | tf_op jit(solution)/shard_map/reshape | solution.py:90
  109.9 65.0 %all-to-all-done.3 = bf16[128,18,432]{2,1,0:T(8,128)(2,1)S(1)} async-done(((bf16[128,18,432]{2,1,0:T(8,128)(2,1)}), bf16[128,18,432]{2,1,0:T(8,128)(2,1)S(1)}, u32[]{:S(2)}, u32[]{:S(2)}) %all-to-all-start.3) | async-done | bytes 1990688 | tf_op jit(solution)/shard_map/all_to_all | solution.py:129
  174.9 8.2 %all-to-all-start = ((bf16[128,3,2304]{2,1,0:T(4,128)(2,1)}), bf16[128,3,2304]{2,1,0:T(4,128)(2,1)}, u32[]{:S(2)}, u32[]{:S(2)}) async-start(bf16[128,3,2304]{2,1,0:T(4,128)(2,1)} %reshape.373), calls=%async_computation | async-start | bytes 4718592 | tf_op jit(solution)/shard_map/all_to_all | solution.py:91
  183.2 2.4 gather_fusion.1
  185.6 54.2 %all-to-all-done = bf16[128,3,2304]{2,1,0:T(4,128)(2,1)} async-done(((bf16[128,3,2304]{2,1,0:T(4,128)(2,1)}), bf16[128,3,2304]{2,1,0:T(4,128)(2,1)}, u32[]{:S(2)}, u32[]{:S(2)}) %all-to-all-start) | async-done | bytes 1769504 | tf_op jit(solution)/shard_map/all_to_all | solution.py:91
  239.8 8.3 %all-to-all-start.4 = ((bf16[128,18,432]{2,1,0:T(8,128)(2,1)}), bf16[128,18,432]{2,1,0:T(8,128)(2,1)S(1)}, u32[]{:S(2)}, u32[]{:S(2)}) async-start(bf16[128,18,432]{2,1,0:T(8,128)(2,1)} %gather_fusion.1), calls=%async_computation.4 | async-start | bytes 6291456 | tf_op jit(solution)/shard_map/all_to_all | solution.py:139
  248.2 5.2 %reshape.374 = bf16[384,2304]{1,0:T(8,128)(2,1)} reshape(bf16[128,3,2304]{2,1,0:T(4,128)(2,1)} %all-to-all-done) | data formatting | bytes 3538944 | tf_op jit(solution)/shard_map/reshape | solution.py:93
  253.4 2.7 fusion.2
  256.1 3.0 convolution_convert_fusion.1
  259.1 5.4 %reshape.375 = bf16[128,3,2304]{2,1,0:T(4,128)(2,1)} reshape(bf16[384,2304]{1,0:T(8,128)(2,1)} %convolution_convert_fusion.1) | data formatting | bytes 3538944 | tf_op jit(solution)/shard_map/reshape | solution.py:104
  264.4 58.0 %all-to-all-done.4 = bf16[128,18,432]{2,1,0:T(8,128)(2,1)S(1)} async-done(((bf16[128,18,432]{2,1,0:T(8,128)(2,1)}), bf16[128,18,432]{2,1,0:T(8,128)(2,1)S(1)}, u32[]{:S(2)}, u32[]{:S(2)}) %all-to-all-start.4) | async-done | bytes 1990688 | tf_op jit(solution)/shard_map/all_to_all | solution.py:139
  322.5 7.8 %all-to-all-start.1 = ((bf16[128,3,2304]{2,1,0:T(4,128)(2,1)}), bf16[128,3,2304]{2,1,0:T(4,128)(2,1)}, u32[]{:S(2)}, u32[]{:S(2)}) async-start(bf16[128,3,2304]{2,1,0:T(4,128)(2,1)} %reshape.375), calls=%async_computation.1 | async-start | bytes 4718592 | tf_op jit(solution)/shard_map/all_to_all | solution.py:105
  330.5 0.7 reshape.367
  331.3 0.7 reshape.369
  332.5 5.2 %reshape.379 = bf16[384,2304]{1,0:T(8,128)(2,1)} reshape(bf16[128,3,2304]{2,1,0:T(4,128)(2,1)} %copy-done.1) | data formatting | bytes 3538944 | tf_op jit(solution)/shard_map/reshape | solution.py:93
  337.7 2.6 squeeze_reshape.3
  340.3 3.1 fusion
  343.4 2.3 convolution_convert_fusion.3
  345.7 5.3 %reshape.381 = bf16[128,3,2304]{2,1,0:T(4,128)(2,1)} reshape(bf16[384,2304]{1,0:T(8,128)(2,1)} %convolution_convert_fusion.3) | data formatting | bytes 3538944 | tf_op jit(solution)/shard_map/reshape | solution.py:104
  351.0 34.1 %all-to-all-done.1 = bf16[128,3,2304]{2,1,0:T(4,128)(2,1)} async-done(((bf16[128,3,2304]{2,1,0:T(4,128)(2,1)}), bf16[128,3,2304]{2,1,0:T(4,128)(2,1)}, u32[]{:S(2)}, u32[]{:S(2)}) %all-to-all-start.1) | async-done | bytes 1769504 | tf_op jit(solution)/shard_map/all_to_all | solution.py:105
  385.1 7.7 %all-to-all-start.5 = ((bf16[128,3,2304]{2,1,0:T(4,128)(2,1)}), bf16[128,3,2304]{2,1,0:T(4,128)(2,1)}, u32[]{:S(2)}, u32[]{:S(2)}) async-start(bf16[128,3,2304]{2,1,0:T(4,128)(2,1)} %reshape.381), calls=%async_computation.5 | async-start | bytes 4718592 | tf_op jit(solution)/shard_map/all_to_all | solution.py:105
  392.8 1.0 fusion.14
  393.8 0.6 add.195
  394.4 0.7 add.182
  395.3 0.7 fusion.36
  396.0 1.7 fusion.49
  397.7 1.5 reshape.384
  399.2 1.1 fusion.15
  400.3 1.3 fusion.8
  401.6 0.7 copy.31
  402.3 1.5 reshape.371
  403.8 0.6 fusion.45
  404.4 0.7 fusion.43
  405.1 0.7 slice_convert_fusion.1
  405.7 5.2 %reshape.376 = bf16[384,2304]{1,0:T(8,128)(2,1)} reshape(bf16[128,3,2304]{2,1,0:T(4,128)(2,1)} %all-to-all-done.1) | data formatting | bytes 3538944 | tf_op jit(solution)/shard_map/reshape | solution.py:106
  410.9 4.1 gather_fusion
  415.0 1.5 convert_reduce_fusion.1
  416.8 32.7 %all-gather = bf16[32,2304]{1,0:T(8,128)(2,1)S(1)} all-gather(bf16[8,2304]{1,0:T(8,128)(2,1)S(1)} %bitcast.105), channel_id=2, replica_groups=mesh['req'=128,'tp'=4] {'tp'}, dimensions={0}, use_global_device_ids=true | all-gather | bytes 184320 | tf_op jit(solution)/shard_map/all_gather | solution.py:116
  449.5 0.8 fusion.37
  450.3 2.6 reshape.383
  452.9 4.1 copy.35
  457.0 4.1 reshape.382
  461.1 1.0 gather_fusion.2
  462.8 10.8 %all-gather.1 = bf16[32,2304]{1,0:T(8,128)(2,1)S(1)} all-gather(bf16[8,2304]{1,0:T(8,128)(2,1)S(1)} %bitcast.106), channel_id=3, replica_groups=mesh['req'=128,'tp'=4] {'tp'}, dimensions={0}, use_global_device_ids=true | all-gather | bytes 184320 | tf_op jit(solution)/shard_map/all_gather | solution.py:116
  473.6 0.8 fusion.38
  474.4 0.6 pad_maximum_fusion
  (65 shorter events, 4.8 us)
Async XLA Ops:
  0.6 395.4 %copy-start = (bf16[256,576]{0,1:T(8,128)(2,1)S(1)}, bf16[256,576]{0,1:T(8,128)(2,1)}, u32[]{:S(2)}) copy-start(bf16[256,576]{0,1:T(8,128)(2,1)} %param.16) | copy-start | bytes 884740
  10.7 79.9 %all-to-all-start.2 = ((bf16[128,3,2304]{2,1,0:T(4,128)(2,1)}), bf16[128,3,2304]{2,1,0:T(4,128)(2,1)S(1)}, u32[]{:S(2)}, u32[]{:S(2)}) async-start(bf16[128,3,2304]{2,1,0:T(4,128)(2,1)} %reshape.378), calls=%async_computation.2 | async-start | bytes 4718592 | tf_op jit(solution)/shard_map/all_to_all | solution.py:91
  40.8 60.8 %copy-start.6 = (s32[128]{0:T(128)S(1)}, s32[128]{0:T(128)}, u32[]{:S(2)}) copy-start(s32[128]{0:T(128)} %param.23) | copy-start | bytes 1540
  90.6 1.4 copy-start.1
  92.1 82.8 %all-to-all-start.3 = ((bf16[128,18,432]{2,1,0:T(8,128)(2,1)}), bf16[128,18,432]{2,1,0:T(8,128)(2,1)S(1)}, u32[]{:S(2)}, u32[]{:S(2)}) async-start(bf16[128,18,432]{2,1,0:T(8,128)(2,1)} %reshape.380), calls=%async_computation.3 | async-start | bytes 6291456 | tf_op jit(solution)/shard_map/all_to_all | solution.py:129
  109.9 73.2 %copy-start.9 = (s32[128]{0:T(128)S(1)}, s32[128]{0:T(128)}, u32[]{:S(2)}) copy-start(s32[128]{0:T(128)} %param.24) | copy-start | bytes 1540
  174.9 65.0 %all-to-all-start = ((bf16[128,3,2304]{2,1,0:T(4,128)(2,1)}), bf16[128,3,2304]{2,1,0:T(4,128)(2,1)}, u32[]{:S(2)}, u32[]{:S(2)}) async-start(bf16[128,3,2304]{2,1,0:T(4,128)(2,1)} %reshape.373), calls=%async_computation | async-start | bytes 4718592 | tf_op jit(solution)/shard_map/all_to_all | solution.py:91
  239.8 82.6 %all-to-all-start.4 = ((bf16[128,18,432]{2,1,0:T(8,128)(2,1)}), bf16[128,18,432]{2,1,0:T(8,128)(2,1)S(1)}, u32[]{:S(2)}, u32[]{:S(2)}) async-start(bf16[128,18,432]{2,1,0:T(8,128)(2,1)} %gather_fusion.1), calls=%async_computation.4 | async-start | bytes 6291456 | tf_op jit(solution)/shard_map/all_to_all | solution.py:139
  264.4 65.9 %copy-start.7 = (s32[1,16]{1,0:T(1,128)S(1)}, s32[1,16]{1,0:T(1,128)}, u32[]{:S(2)}) copy-start(s32[1,16]{1,0:T(1,128)} %param.18) | copy-start | bytes 196
  264.4 66.1 %copy-start.4 = (bf16[2,8,576]{2,1,0:T(8,128)(2,1)S(1)}, bf16[2,8,576]{2,1,0:T(8,128)(2,1)}, u32[]{:S(2)}) copy-start(bf16[2,8,576]{2,1,0:T(8,128)(2,1)} %param.13) | copy-start | bytes 55300
  264.4 66.8 %copy-start.5 = (bf16[2,8,576]{2,1,0:T(8,128)(2,1)S(1)}, bf16[2,8,576]{2,1,0:T(8,128)(2,1)}, u32[]{:S(2)}) copy-start(bf16[2,8,576]{2,1,0:T(8,128)(2,1)} %param.14) | copy-start | bytes 55300
  264.4 68.1 %copy-start.8 = (f32[2,8,2]{1,2,0:T(2,128)S(1)}, f32[2,8,2]{1,2,0:T(2,128)}, u32[]{:S(2)}) copy-start(f32[2,8,2]{1,2,0:T(2,128)} %param.22) | copy-start | bytes 388
  322.5 62.6 %all-to-all-start.1 = ((bf16[128,3,2304]{2,1,0:T(4,128)(2,1)}), bf16[128,3,2304]{2,1,0:T(4,128)(2,1)}, u32[]{:S(2)}, u32[]{:S(2)}) async-start(bf16[128,3,2304]{2,1,0:T(4,128)(2,1)} %reshape.375), calls=%async_computation.1 | async-start | bytes 4718592 | tf_op jit(solution)/shard_map/all_to_all | solution.py:105
  340.3 3.1 copy-start.2
  385.1 72.0 %all-to-all-start.5 = ((bf16[128,3,2304]{2,1,0:T(4,128)(2,1)}), bf16[128,3,2304]{2,1,0:T(4,128)(2,1)}, u32[]{:S(2)}, u32[]{:S(2)}) async-start(bf16[128,3,2304]{2,1,0:T(4,128)(2,1)} %reshape.381), calls=%async_computation.5 | async-start | bytes 4718592 | tf_op jit(solution)/shard_map/all_to_all | solution.py:105
  392.8 12.3 %copy-start.3 = (bf16[2,8,2304]{2,1,0:T(8,128)(2,1)S(1)}, bf16[2,8,2304]{2,1,0:T(8,128)(2,1)}, u32[]{:S(2)}) copy-start(bf16[2,8,2304]{2,1,0:T(8,128)(2,1)} %param.19) | copy-start | bytes 221188
